TPU v7x, 256 devices: a whole 4x4x8 slice. The times are simulated.
256 devices in a mesh: feat: 64 (over x, y_hi, z), tgt: 4 (over y_lo, core).
Axes of the slice: x: 4, y: 4 (y_hi: 2, y_lo: 2; y = y_hi * 2 + y_lo), z: 8, core: 2. Of those that a mesh axis runs over, the one named last changes fastest.
Arguments:
- sources: bfloat16 [4, 128, 2304], P('tgt'), may hold values from -6 to 6
- targets: bfloat16 [4, 128, 2304], P('tgt', 'feat'), may hold values from -6 to 6
- enc_weight: bfloat16 [4, 2304, 16384], P('tgt', None, 'feat'), may hold values from -0.125 to 0.125
- enc_bias: float32 [4, 16384], P('tgt', 'feat'), may hold values from -5 to 5
- dec_weight: bfloat16 [4, 4, 16384, 2304], P('tgt', None, 'feat'), may hold values from -0.046875 to 0.046875
- pair_mask: int32 [4, 4], replicated, may hold values from 0 to 1, as said below
Outputs:
- error: bfloat16 [4, 128, 2304], P('tgt', 'feat')
- latent_grad: bfloat16 [4, 128, 16384], P('tgt', None, 'feat')
Inputs may be any that keep to these rules, and one draw needn't show every extreme that they name: pair_mask[t, s] is 0 wherever s > t and 1 wherever s == t.
All inputs are finite; a program needn't handle non-finite values.
Results may differ from a plain program's by a relative error of at most 0.0055.
Values may be sent and summed in bfloat16 or wider, within the bound.
No kernel may reach another device: no remote copies, remote signals or barrier semaphores. Data moves between devices by JAX's collectives and lax.ppermute only.
A program may use at most 64 MiB of HBM per device.

v0:
```python
import jax
import jax.numpy as jnp
from jax import lax
from jax.sharding import PartitionSpec as P


def per_device(sources, targets, enc_weight, enc_bias, dec_weight, pair_mask):
    layer_count = dec_weight.shape[1]
    width = sources.shape[2]
    rows_local = targets.shape[1]
    pre = jnp.dot(sources[0], enc_weight[0], preferred_element_type=jnp.float32) + enc_bias[0]
    latent = jnp.maximum(pre, 0.0).astype(jnp.bfloat16)
    latent_all = lax.all_gather(latent[None], "tgt", axis=0, tiled=True)
    owner = lax.axis_index("tgt")
    mask_row = lax.dynamic_index_in_dim(pair_mask, owner, 0, keepdims=False)
    total = jnp.zeros((rows_local * lax.axis_size("feat"), width), jnp.float32)
    for recon_source in range(layer_count):
        rows = latent_all[recon_source]
        recon_weight = mask_row[recon_source].astype(jnp.float32)
        total = total + recon_weight * jnp.dot(
            rows, dec_weight[0, recon_source], preferred_element_type=jnp.float32
        )
    share = lax.psum_scatter(total, "feat", scatter_dimension=0, tiled=True)
    err_local = (share - targets[0].astype(jnp.float32)).astype(jnp.bfloat16)
    err_full = lax.all_gather(err_local, "feat", axis=0, tiled=True)
    terms = []
    for source in range(layer_count):
        weight = mask_row[source].astype(jnp.float32)
        term = weight * lax.dot_general(
            err_full,
            dec_weight[0, source],
            (((1,), (1,)), ((), ())),
            preferred_element_type=jnp.float32,
        )
        terms.append(term)
    stacked = jnp.stack(terms)
    grads = lax.psum_scatter(stacked, "tgt", scatter_dimension=0, tiled=True)
    return (err_local[None], grads.astype(jnp.bfloat16))


def solution(mesh):
    in_specs = (
        P("tgt", None, None),
        P("tgt", "feat", None),
        P("tgt", None, "feat"),
        P("tgt", "feat"),
        P("tgt", None, "feat", None),
        P(),
    )
    out_specs = (P("tgt", "feat", None), P("tgt", None, "feat"))
    return jax.shard_map(
        per_device, mesh=mesh, in_specs=in_specs, out_specs=out_specs, check_vma=False
    )
```

profile of v0, /device:TPU:1, one launch (start us, length us, event | category | flops | bytes accessed | tf_op | source)
XLA Modules:
  0.0 911.5 jit_solution(5537049860476209958)
XLA Ops:
  7.2 0.0 all-reduce.3.cloned.1.call-start
  7.2 0.8 constant_dynamic-slice_fusion
  8.0 0.7 fusion.65
  9.2 1.4 fusion.47
  10.7 8.8 all-gather
  21.5 1.8 convolution_multiply_fusion.3
  23.2 1.6 fusion.2
  24.9 0.3 fusion.1
  25.2 1.4 fusion
  26.6 0.0 all-reduce.3.cloned.1.call-update
  26.6 0.0 reduce-scatter.2.cloned.1.call-start
  26.6 0.6 copy-done.4
  27.2 0.6 dynamic-slice
  28.5 633.8 %all-reduce.3.cloned.1.call-done = f32[128,2304]{1,0:T(8,128)} async-done(((f32[128,2304]{1,0:T(8,128)}), f32[128,2304]{1,0:T(8,128)}) %all-reduce.3.cloned.1.call-update) | async-done | bytes 1179664
  662.3 0.9 fusion.64
  663.2 155.4 %all-gather.1 = bf16[64,2,2304]{2,1,0:T(2,128)(2,1)S(1)} all-gather(bf16[1,2,2304]{2,1,0:T(2,128)(2,1)S(1)} %fusion.64), channel_id=1, replica_groups=mesh['feat'=64,'tgt'=4] {'feat'}, dimensions={0}, use_global_device_ids=true | all-gather | bytes 599040 | tf_op jit(solution)/shard_map/all_gather | solution.py:25
  818.6 0.2 reshape.29
  818.8 1.8 fusion.26
  820.6 1.8 fusion.32
  822.4 1.8 fusion.38
  824.3 1.8 fusion.44
  826.1 0.8 pad_maximum_fusion
  827.0 76.1 %reduce-scatter.2.cloned.1.call-done = f32[1,128,256]{2,1,0:T(8,128)} async-done(((f32[4,128,256]{2,1,0:T(8,128)}), f32[1,128,256]{2,1,0:T(8,128)}) %reduce-scatter.2.cloned.1.call-update) | async-done | bytes 131088 | tf_op jit(solution)/shard_map/reduce_scatter | solution.py:37
  903.1 1.5 convert_element_type.55
  (10 shorter events, 0.0 us)
Async XLA Ops:
  7.2 2.1 copy-start
  7.2 655.1 %all-reduce.3.cloned.1.call-start = ((), (), s32[]{:S(2)}) async-start(), calls=%async_computation.2 | async-start | bytes 2359296
  21.5 3.4 copy-start.1
  26.6 0.7 copy-start.4
  26.6 635.7 %copy-start.3 = (bf16[1,2,2304]{2,1,0:T(2,128)(2,1)S(1)}, bf16[1,2,2304]{2,1,0:T(2,128)(2,1)}, u32[]{:S(2)}) copy-start(bf16[1,2,2304]{2,1,0:T(2,128)(2,1)} %param.7) | copy-start | bytes 27652
  26.6 876.5 %reduce-scatter.2.cloned.1.call-start = ((), (), s32[]{:S(2)}) async-start(), calls=%async_computation.1 | async-start | bytes 655360 | tf_op jit(solution)/shard_map/reduce_scatter | solution.py:37
  663.2 157.5 %copy-start.2 = (bf16[1,2,2304]{2,1,0:T(2,128)(2,1)}, bf16[1,2,2304]{2,1,0:T(2,128)(2,1)S(1)}, u32[]{:S(2)}) copy-start(bf16[1,2,2304]{2,1,0:T(2,128)(2,1)S(1)} %fusion.64) | copy-start | bytes 27652
Sparse Core Ops, SparseCore 0:
  26.7 635.5 all-reduce.2
  827.1 75.9 reduce-scatter.1
where the time goes:
time: 912 us; the launch traced here: 911 us
  waiting for transfers between devices  710 us (78%)
  blocking collectives  164 us (18%)
  between operations  17.4 us (2%)
  matrix products  13.7 us (2%)
    unnamed x3, waiting for transfers between devices  634 us
    all_gather x1, blocking collectives, per_device(): err_full = lax.all_gather(err_local, 'feat', axis=0, tiled=True)  155 us
    reduce_scatter x1, waiting for transfers between devices, per_device(): grads = lax.psum_scatter(stacked, 'tgt', scatter_dimension=0, tiled=True)  76.1 us
  transfers between devices with their start and end apart: 2, of which 2 were waited for; matrix products, arithmetic and copies ran while one was open for 0% of the time, Pallas kernels for 0%

commit v1 on v0

--- a/solution.py
+++ b/solution.py
@@ -22,7 +22,10 @@
         )
     share = lax.psum_scatter(total, "feat", scatter_dimension=0, tiled=True)
     err_local = (share - targets[0].astype(jnp.float32)).astype(jnp.bfloat16)
-    err_full = lax.all_gather(err_local, "feat", axis=0, tiled=True)
+    count = lax.axis_size("feat")
+    parts = jnp.stack([err_local for _ in range(count)])
+    parts = lax.all_to_all(parts, "feat", split_axis=0, concat_axis=0)
+    err_full = jnp.concatenate(parts, axis=0)
     terms = []
     for source in range(layer_count):
         weight = mask_row[source].astype(jnp.float32)

time: 912 us -> 756 us (0.83)
  blocking collectives: 164 us -> 31.1 us
  waiting for transfers between devices: 710 us -> 687 us
    all_gather x1 -> x0, blocking collectives: 155 us -> none  [per_device(): err_full = lax.all_gather(err_local, 'feat', axis=0, tiled=True)]
    reduce_scatter x1, waiting for transfers between devices: 76.1 us -> 53.4 us  [per_device(): grads = lax.psum_scatter(stacked, 'tgt', scatter_dimension=0, tiled=True)]
    all_to_all x0 -> x1, blocking collectives: none -> 22.3 us  [per_device(): parts = lax.all_to_all(parts, 'feat', split_axis=0, concat_axis=0)]
where the time goes in v1:
time: 756 us
  waiting for transfers between devices  687 us (91%)
  blocking collectives  31.1 us (4%)
  between operations  17.4 us (2%)
  matrix products  13.7 us (2%)
    unnamed x3, waiting for transfers between devices  634 us
    reduce_scatter x1, waiting for transfers between devices, per_device(): grads = lax.psum_scatter(stacked, 'tgt', scatter_dimension=0, tiled=True)  53.4 us
    all_to_all x1, blocking collectives, per_device(): parts = lax.all_to_all(parts, 'feat', split_axis=0, concat_axis=0)  22.3 us
  transfers between devices with their start and end apart: 2, of which 2 were waited for; matrix products, arithmetic and copies ran while one was open for 0% of the time, Pallas kernels for 0%

profile of v1, /device:TPU:1, one launch (start us, length us, event | category | flops | bytes accessed | tf_op | source)
XLA Modules:
  0.0 756.0 jit_solution(9417950259763940476)
XLA Ops:
  7.2 0.0 all-reduce.3.cloned.1.call-start
  7.2 0.8 constant_dynamic-slice_fusion
  8.0 0.7 fusion.64
  9.2 1.4 fusion.47
  10.7 8.8 %all-gather = bf16[512,256]{1,0:T(8,128)(2,1)S(1)} all-gather(bf16[128,256]{1,0:T(8,128)(2,1)S(1)} %fusion.47), channel_id=2, replica_groups=mesh['feat'=64,'tgt'=4] {'tgt'}, dimensions={0}, use_global_device_ids=true | all-gather | bytes 327680 | tf_op jit(solution)/shard_map/all_gather | solution.py:13
  21.5 1.8 convolution_multiply_fusion.3
  23.2 1.6 fusion.2
  24.9 0.3 fusion.1
  25.2 1.4 fusion
  26.6 0.0 reduce-scatter.2.cloned.1.call-start
  26.6 0.6 copy-done.4
  27.2 0.6 dynamic-slice
  28.5 633.8 %all-reduce.3.cloned.1.call-done = f32[128,2304]{1,0:T(8,128)} async-done(((f32[128,2304]{1,0:T(8,128)}), f32[128,2304]{1,0:T(8,128)}) %all-reduce.3.cloned.1.call-update) | async-done | bytes 1179664
  662.3 0.9 fusion.63
  663.2 0.3 stack.12
  663.5 22.3 %all_to_all.5 = bf16[64,2,2304]{2,1,0:T(2,128)(2,1)S(1)} all-to-all(bf16[64,2,2304]{2,1,0:T(2,128)(2,1)S(1)} %stack.12), channel_id=1, replica_groups=mesh['feat'=64,'tgt'=4] {'feat'}, dimensions={0} | all-to-all | bytes 1179648 | tf_op jit(solution)/shard_map/all_to_all | solution.py:27
  685.8 0.2 reshape.23
  686.0 1.8 fusion.26
  687.9 1.8 fusion.32
  689.7 1.8 fusion.38
  691.5 1.8 fusion.44
  693.3 0.8 pad_maximum_fusion
  694.2 53.4 %reduce-scatter.2.cloned.1.call-done = f32[1,128,256]{2,1,0:T(8,128)} async-done(((f32[4,128,256]{2,1,0:T(8,128)}), f32[1,128,256]{2,1,0:T(8,128)}) %reduce-scatter.2.cloned.1.call-update) | async-done | bytes 131088 | tf_op jit(solution)/shard_map/reduce_scatter | solution.py:40
  747.6 1.5 convert_element_type.55
  (11 shorter events, 0.1 us)
Async XLA Ops:
  7.2 2.1 copy-start
  7.2 655.1 %all-reduce.3.cloned.1.call-start = ((), (), s32[]{:S(2)}) async-start(), calls=%async_computation.3 | async-start | bytes 2359296
  21.5 3.4 copy-start.1
  26.6 0.7 copy-start.4
  26.6 635.7 %copy-start.3 = (bf16[1,2,2304]{2,1,0:T(2,128)(2,1)S(1)}, bf16[1,2,2304]{2,1,0:T(2,128)(2,1)}, u32[]{:S(2)}) copy-start(bf16[1,2,2304]{2,1,0:T(2,128)(2,1)} %param.7) | copy-start | bytes 27652
  26.6 721.0 %reduce-scatter.2.cloned.1.call-start = ((), (), s32[]{:S(2)}) async-start(), calls=%async_computation.2 | async-start | bytes 655360 | tf_op jit(solution)/shard_map/reduce_scatter | solution.py:40
  663.2 22.9 %copy-start.2 = (bf16[2,2304]{1,0:T(2,128)(2,1)}, bf16[2,2304]{1,0:T(2,128)(2,1)S(1)}, u32[]{:S(2)}) copy-start(bf16[2,2304]{1,0:T(2,128)(2,1)S(1)} %fusion.63) | copy-start | bytes 27652
Sparse Core Ops, SparseCore 0:
  26.7 635.5 all-reduce.2
  694.3 53.2 reduce-scatter.1
